TPU v7x, 32 devices: a whole 2x2x4 slice. The times are simulated.
32 devices in a mesh: dp: 8 (over z, x), seq: 4 (over y, core).
Axes of the slice: x: 2, y: 2, z: 4, core: 2. Of those that a mesh axis runs over, the one named last changes fastest.
Arguments:
- queries: bfloat16 [8, 512, 1024], P('dp', 'seq'), may hold values from -6 to 6
- key_vecs: bfloat16 [8, 512, 1024], P('dp', 'seq'), may hold values from -6 to 6
- value_vecs: bfloat16 [8, 512, 1024], P('dp', 'seq'), may hold values from -6 to 6
- residual_in: bfloat16 [8, 512, 1024], P('dp', 'seq'), may hold values from -8 to 8
- point_weight: bfloat16 [1024, 2048], P('seq'), may hold values from -0.5 to 0.5
- context_grad: bfloat16 [8, 512, 1024], P('dp', 'seq'), may hold values from -6 to 6
- depth_kernel: float32 [31, 1024], replicated, may hold values from -1 to 1
- norm_gain: float32 [1024], replicated, may hold values from 0.5 to 1.5
- norm_bias: float32 [1024], replicated, may hold values from -3 to 3
- conv_grad: bfloat16 [8, 512, 1024], P('dp', 'seq'), may hold values from -1.5 to 1.5
Outputs:
- context: bfloat16 [8, 512, 1024], P('dp', 'seq')
- conv_output: bfloat16 [8, 512, 1024], P('dp', 'seq')
- query_grad: bfloat16 [8, 512, 1024], P('dp', 'seq')
- key_grad: bfloat16 [8, 512, 1024], P('dp', 'seq')
- value_grad: bfloat16 [8, 512, 1024], P('dp', 'seq')
- input_grad: bfloat16 [8, 512, 2048], P('dp', 'seq')
- residual_grad: bfloat16 [8, 512, 1024], P('dp', 'seq')
- kernel_grad: float32 [31, 1024], replicated
- gain_grad: float32 [1024], replicated
- bias_grad: float32 [1024], replicated
All inputs are finite; a program needn't handle non-finite values.
Results may differ from a plain program's by a relative error of at most 0.0049.
The roundings to bfloat16 on the way count: a program that leaves them out, or rounds other values in their place, can miss the bound.
Values may be sent and summed in bfloat16 or wider, within the bound.
A program may use at most 64 MiB of HBM per device.

v0:
```python
import jax
import jax.numpy as jnp
from jax import lax
from jax.sharding import PartitionSpec as P

HEADS = 16


def from_behind(block, axis, distance):
    devices = range(lax.axis_size(axis))
    route = [(i - distance, i) for i in devices if i - distance in devices]
    return lax.ppermute(block, axis, route)


def block_probs(query_block, key_heads, scaling):
    scores = (
        jnp.einsum("qhd,khd->hqk", query_block, key_heads, preferred_element_type=jnp.float32)
        * scaling
    )
    shifted = jnp.exp(scores - jnp.max(scores, axis=2, keepdims=True))
    return shifted / jnp.sum(shifted, axis=2, keepdims=True)


def attend_forward(query_part, key_part, value_part, head_count):
    frames, channels = query_part.shape
    head_depth = channels // head_count
    scaling = head_depth ** (-0.5)
    query_heads = query_part.reshape(frames, head_count, head_depth)
    key_heads = key_part.reshape(frames, head_count, head_depth)
    value_heads = value_part.reshape(frames, head_count, head_depth)
    block_rows = min(512, frames)

    def one_block(running, index):
        query_block = lax.dynamic_slice_in_dim(query_heads, index * block_rows, block_rows, 0)
        rounded = block_probs(query_block, key_heads, scaling).astype(jnp.bfloat16)
        context = jnp.einsum(
            "hqk,khd->qhd", rounded, value_heads, preferred_element_type=jnp.float32
        ).astype(jnp.bfloat16)
        return (running, context)

    unused, blocks = lax.scan(
        one_block, jnp.zeros((), jnp.float32), jnp.arange(frames // block_rows)
    )
    return blocks.reshape(frames, channels)


def attend_backward(query_part, key_part, value_part, grad_part, context_part, head_count):
    frames, channels = query_part.shape
    head_depth = channels // head_count
    scaling = head_depth ** (-0.5)
    query_heads = query_part.reshape(frames, head_count, head_depth)
    key_heads = key_part.reshape(frames, head_count, head_depth)
    value_heads = value_part.reshape(frames, head_count, head_depth)
    grad_heads = grad_part.reshape(frames, head_count, head_depth)
    context_heads = context_part.reshape(frames, head_count, head_depth)
    block_rows = min(512, frames)

    def one_block(running, index):
        key_total, value_total = running
        start = index * block_rows
        query_block = lax.dynamic_slice_in_dim(query_heads, start, block_rows, 0)
        grad_block = lax.dynamic_slice_in_dim(grad_heads, start, block_rows, 0)
        context_block = lax.dynamic_slice_in_dim(context_heads, start, block_rows, 0)
        probabilities = block_probs(query_block, key_heads, scaling)
        rounded = probabilities.astype(jnp.bfloat16)
        row_dots = jnp.sum(
            grad_block.astype(jnp.float32) * context_block.astype(jnp.float32), axis=2
        )
        prob_grad = jnp.einsum(
            "qhd,khd->hqk", grad_block, value_heads, preferred_element_type=jnp.float32
        )
        score_grad = (probabilities * (prob_grad - row_dots.T[:, :, None]) * scaling).astype(
            jnp.bfloat16
        )
        query_grad = jnp.einsum(
            "hqk,khd->qhd", score_grad, key_heads, preferred_element_type=jnp.float32
        ).astype(jnp.bfloat16)
        key_total = key_total + jnp.einsum(
            "hqk,qhd->khd", score_grad, query_block, preferred_element_type=jnp.float32
        )
        value_total = value_total + jnp.einsum(
            "hqk,qhd->khd", rounded, grad_block, preferred_element_type=jnp.float32
        )
        return ((key_total, value_total), query_grad)

    empty = jnp.zeros((frames, head_count, head_depth), jnp.float32)
    totals, blocks = lax.scan(one_block, (empty, empty), jnp.arange(frames // block_rows))
    query_grad = blocks.reshape(frames, channels)
    key_grad = totals[0].astype(jnp.bfloat16).reshape(frames, channels)
    value_grad = totals[1].astype(jnp.bfloat16).reshape(frames, channels)
    return (query_grad, key_grad, value_grad)


def shards(
    queries,
    key_vecs,
    value_vecs,
    residual_in,
    point_weight,
    context_grad,
    depth_kernel,
    norm_gain,
    norm_bias,
    conv_grad,
):
    head_count = HEADS // lax.axis_size("seq")
    query_heads, key_heads, value_heads = (
        lax.all_to_all(queries, "seq", split_axis=2, concat_axis=1, tiled=True),
        lax.all_to_all(key_vecs, "seq", split_axis=2, concat_axis=1, tiled=True),
        lax.all_to_all(value_vecs, "seq", split_axis=2, concat_axis=1, tiled=True),
    )
    context_local = attend_forward(query_heads[0], key_heads[0], value_heads[0], head_count)
    context_out = lax.all_to_all(
        context_local[None], "seq", split_axis=1, concat_axis=2, tiled=True
    )
    taps = depth_kernel.shape[0]
    channels = depth_kernel.shape[1]
    span = taps - 1
    frames = residual_in.shape[1]
    mixed = (residual_in[0].astype(jnp.float32) + context_out[0].astype(jnp.float32)).astype(
        jnp.bfloat16
    )
    pre_conv = jnp.dot(
        mixed,
        lax.all_gather(point_weight, "seq", axis=0, tiled=True),
        preferred_element_type=jnp.float32,
    )
    conv_input = pre_conv.astype(jnp.bfloat16)[None]
    value_half = conv_input[:, :, :channels].astype(jnp.float32)
    gate_sig = jax.nn.sigmoid(conv_input[:, :, channels:].astype(jnp.float32))
    glu = (value_half * gate_sig).astype(jnp.bfloat16)
    earlier = from_behind(glu[:, frames - span :], "seq", 1)
    glu_wide = jnp.concatenate([earlier, glu], axis=1)
    glu_view = lax.optimization_barrier(glu_wide).astype(jnp.float32)
    depthwise = jnp.zeros((1, frames, channels), jnp.float32)
    for offset in range(taps):
        depthwise = depthwise + depth_kernel[offset] * glu_view[:, offset : offset + frames]
    average = jnp.mean(depthwise, axis=2, keepdims=True)
    centered = depthwise - average
    variance = jnp.mean(centered * centered, axis=2, keepdims=True)
    inverse = lax.rsqrt(variance + 1e-05)
    normed = centered * inverse
    affine = normed * norm_gain + norm_bias
    sig_affine = jax.nn.sigmoid(affine)
    conv_output = (affine * sig_affine).astype(jnp.bfloat16)
    affine_grad = conv_grad.astype(jnp.float32) * (sig_affine * (1.0 + affine * (1.0 - sig_affine)))
    gain_term = jnp.sum(affine_grad * normed, axis=(0, 1))
    bias_term = jnp.sum(affine_grad, axis=(0, 1))
    normed_grad = affine_grad * norm_gain
    depth_grad = inverse * (
        normed_grad
        - jnp.mean(normed_grad, axis=2, keepdims=True)
        - normed * jnp.mean(normed_grad * normed, axis=2, keepdims=True)
    )
    kernel_term = jnp.stack(
        [
            jnp.sum(depth_grad * glu_view[:, offset : offset + frames], axis=(0, 1))
            for offset in range(taps)
        ]
    )
    kernel_total, gain_total, bias_total = lax.psum(
        (kernel_term, gain_term, bias_term), ("dp", "seq")
    )
    recordings = lax.axis_size("dp")
    kernel_grad = kernel_total / recordings
    gain_grad = gain_total / recordings
    bias_grad = bias_total / recordings
    later = from_behind(depth_grad[:, :span], "seq", -1)
    grad_wide = jnp.concatenate([depth_grad, later], axis=1)
    glu_grad = jnp.zeros((1, frames, channels), jnp.float32)
    for offset in range(taps):
        begin = span - offset
        glu_grad = glu_grad + depth_kernel[offset] * grad_wide[:, begin : begin + frames]
    input_grad = jnp.concatenate(
        [glu_grad * gate_sig, glu_grad * value_half * gate_sig * (1.0 - gate_sig)], axis=2
    ).astype(jnp.bfloat16)
    slope_rows = input_grad[0]
    mixed_grad = jnp.einsum(
        "fc,dc->fd",
        slope_rows,
        lax.all_gather(point_weight, "seq", axis=0, tiled=True),
        preferred_element_type=jnp.float32,
    )
    residual_grad = (context_grad.astype(jnp.float32) + mixed_grad[None]).astype(jnp.bfloat16)
    grad_heads = lax.all_to_all(residual_grad, "seq", split_axis=2, concat_axis=1, tiled=True)
    query_grad, key_grad, value_grad = attend_backward(
        query_heads[0], key_heads[0], value_heads[0], grad_heads[0], context_local, head_count
    )
    query_out, key_out, value_out = (
        lax.all_to_all(query_grad[None], "seq", split_axis=1, concat_axis=2, tiled=True),
        lax.all_to_all(key_grad[None], "seq", split_axis=1, concat_axis=2, tiled=True),
        lax.all_to_all(value_grad[None], "seq", split_axis=1, concat_axis=2, tiled=True),
    )
    return (
        context_out,
        conv_output,
        query_out,
        key_out,
        value_out,
        input_grad,
        residual_grad,
        kernel_grad,
        gain_grad,
        bias_grad,
    )


def solution(mesh):
    in_specs = (
        P("dp", "seq", None),
        P("dp", "seq", None),
        P("dp", "seq", None),
        P("dp", "seq", None),
        P("seq", None),
        P("dp", "seq", None),
        P(),
        P(),
        P(),
        P("dp", "seq", None),
    )
    out_specs = (
        P("dp", "seq", None),
        P("dp", "seq", None),
        P("dp", "seq", None),
        P("dp", "seq", None),
        P("dp", "seq", None),
        P("dp", "seq", None),
        P("dp", "seq", None),
        P(),
        P(),
        P(),
    )
    return jax.shard_map(shards, mesh=mesh, in_specs=in_specs, out_specs=out_specs, check_vma=False)
```

profile of v0, /device:TPU:0, one launch (start us, length us, event | category | flops | bytes accessed | tf_op | source)
XLA Modules:
  0.0 264.9 jit_solution(9525014765251899373)
XLA Ops:
  7.9 1.3 copy.72
  9.8 2.3 reduce.5
  12.9 4.2 %all-to-all-start = ((bf16[4,2,16384]{2,1,0:T(2,128)(2,1)}), bf16[4,2,16384]{2,1,0:T(2,128)(2,1)S(1)}, u32[]{:S(2)}, u32[]{:S(2)}) async-start(bf16[4,2,16384]{2,1,0:T(2,128)(2,1)} %reshape.213), calls=%async_computation | async-start | bytes 524288 | tf_op jit(solution)/shard_map/all_to_all | solution.py:108
  17.1 1.3 copy.74
  18.4 2.3 reduce.6
  21.4 2.4 all-to-all-done
  23.9 3.4 %all-to-all-start.1 = ((bf16[4,2,16384]{2,1,0:T(2,128)(2,1)}), bf16[4,2,16384]{2,1,0:T(2,128)(2,1)S(1)}, u32[]{:S(2)}, u32[]{:S(2)}) async-start(bf16[4,2,16384]{2,1,0:T(2,128)(2,1)} %reshape.215), calls=%async_computation.1 | async-start | bytes 524288 | tf_op jit(solution)/shard_map/all_to_all | solution.py:109
  27.7 2.3 reduce.4
  30.7 5.7 %all-to-all-done.1 = bf16[4,2,16384]{2,1,0:T(2,128)(2,1)S(1)} async-done(((bf16[4,2,16384]{2,1,0:T(2,128)(2,1)}), bf16[4,2,16384]{2,1,0:T(2,128)(2,1)S(1)}, u32[]{:S(2)}, u32[]{:S(2)}) %all-to-all-start.1) | async-done | bytes 262176 | tf_op jit(solution)/shard_map/all_to_all | solution.py:109
  36.4 3.4 %all-to-all-start.2 = ((bf16[4,2,16384]{2,1,0:T(2,128)(2,1)}), bf16[4,2,16384]{2,1,0:T(2,128)(2,1)S(1)}, u32[]{:S(2)}, u32[]{:S(2)}) async-start(bf16[4,2,16384]{2,1,0:T(2,128)(2,1)} %reshape.211), calls=%async_computation.2 | async-start | bytes 524288 | tf_op jit(solution)/shard_map/all_to_all | solution.py:110
  42.0 7.0 %all-to-all-done.2 = bf16[4,2,16384]{2,1,0:T(2,128)(2,1)S(1)} async-done(((bf16[4,2,16384]{2,1,0:T(2,128)(2,1)}), bf16[4,2,16384]{2,1,0:T(2,128)(2,1)S(1)}, u32[]{:S(2)}, u32[]{:S(2)}) %all-to-all-start.2) | async-done | bytes 262176 | tf_op jit(solution)/shard_map/all_to_all | solution.py:110
  49.6 3.5 %fusion.114 = (f32[4,512]{1,0:T(4,128)S(1)}, f32[4,512,512]{1,2,0:T(8,128)}) fusion(bf16[512,4,64]{0,2,1:T(8,128)(2,1)S(1)} %reshape_squeeze.15, bf16[512,4,64]{0,2,1:T(8,128)(2,1)S(1)} %reshape_squeeze.16), kind=kOutput, calls=%fused_computation.236 | convolution fusion | flops 137363968 | bytes 4726784 | tf_op jit(solution)/shard_map/while/body/eval_jaxpr/sub | solution.py:20
  53.1 2.8 %fusion.6 = bf16[4,512,512]{1,2,0:T(8,128)(2,1)S(1)} fusion(f32[4,512,512]{1,2,0:T(8,128)} %get-tuple-element.138, f32[4,512]{1,0:T(4,128)S(1)} %get-tuple-element.137), kind=kLoop, calls=%fused_computation.38 | loop fusion | flops 2097152 | bytes 6299648 | tf_op jit(solution)/shard_map/while/body/eval_jaxpr/convert_element_type | solution.py:35
  56.8 2.3 reduce.7
  59.8 3.6 %all-to-all-start.3 = ((bf16[4,2,16384]{2,1,0:T(2,128)(2,1)}), bf16[4,2,16384]{2,1,0:T(2,128)(2,1)S(1)}, u32[]{:S(2)}, u32[]{:S(2)}) async-start(bf16[4,2,16384]{2,1,0:T(2,128)(2,1)} %reshape.217), calls=%async_computation.3 | async-start | bytes 524288 | tf_op jit(solution)/shard_map/all_to_all | solution.py:113
  64.2 5.1 %all-to-all-done.3 = bf16[4,2,16384]{2,1,0:T(2,128)(2,1)S(1)} async-done(((bf16[4,2,16384]{2,1,0:T(2,128)(2,1)}), bf16[4,2,16384]{2,1,0:T(2,128)(2,1)S(1)}, u32[]{:S(2)}, u32[]{:S(2)}) %all-to-all-start.3) | async-done | bytes 262176 | tf_op jit(solution)/shard_map/all_to_all | solution.py:113
  69.7 1.1 fusion.105
  70.8 2.9 %fusion.4 = bf16[1,128,2048]{2,1,0:T(8,128)(2,1)S(1)} fusion(bf16[128,1024]{0,1:T(8,128)(2,1)S(1)} %fusion.105, bf16[1024,2048]{1,0:T(8,128)(2,1)} %all-gather.2.cloned.1.call-done), kind=kOutput, calls=%fused_computation.35 | convolution fusion | flops 537133056 | bytes 4980736 | tf_op jit(solution)/shard_map/dot_general | solution.py:123
  74.5 2.2 collective-permute-start
  78.2 1.8 copy.95
  81.0 3.2 %fusion.111 = (f32[128]{0:T(128)S(1)}, f32[1,128,1024]{2,1,0:T(8,128)S(1)}) fusion(f32[1,158,1024]{2,1,0:T(8,128)S(1)} %convert_element_type.110, f32[1024]{0:T(1024)} %bitcast.253, f32[1024]{0:T(1024)} %bitcast.255, f32[1024]{0:T(1024)S(1)} %bitcast.197, f32[1024]{0:T(1024)S(1)} %bitcast.199, f32[1024]{0:T(1024)S(1)} %bitcast.201, f32[1024]{0:T(1024)} %bitcast.203, ...), kind=kLoop, calls=%fused_computation.233 | loop fusion | flops 8126336 | bytes 16904704 | tf_op jit(solution)/shard_map/reduce_sum | solution.py:138
  84.5 1.8 multiply_reduce_fusion.1
  86.2 1.3 multiply_reduce_fusion.2
  89.0 2.6 stack.127
  91.6 1.3 collective-permute-start.1
  92.9 43.4 %all-reduce = (f32[1024]{0:T(1024)}, f32[1024]{0:T(1024)}) all-reduce(f32[1024]{0:T(1024)} %get-tuple-element.93, f32[1024]{0:T(1024)} %get-tuple-element.96), channel_id=1, replica_groups=mesh['dp'=8,'seq'=4] {'dp','seq'}, use_global_device_ids=true, to_apply=%region_40.41 | all-reduce | flops 2048 | bytes 16384 | tf_op jit(solution)/shard_map/psum | solution.py:161
  136.3 1.3 broadcast_multiply_fusion.1
  137.6 3.6 %multiply_convert_fusion.1 = (bf16[1,128,1024]{2,1,0:T(8,128)(2,1)S(1)}, f32[1,128,1024]{2,1,0:T(8,128)S(1)}) fusion(bf16[1,128,2048]{2,1,0:T(8,128)(2,1)S(1)} %fusion.4, f32[1,128,1024]{2,1,0:T(8,128)S(1)} %get-tuple-element.99, f32[1024]{0:T(1024)} %bitcast.254, f32[1,30,1024]{2,1,0:T(8,128)S(1)} %collective-permute-done.1, f32[1024]{0:T(1024)} %bitcast.256, ...), kind=kLoop, calls=%fused_computation.210 | loop fusion | flops 12713984 | bytes 1822720 | tf_op jit(solution)/shard_map/convert.7
  141.9 3.7 %fusion.8 = bf16[1,128,1024]{2,1,0:T(8,128)(2,1)S(1)} fusion(bf16[1024,2048]{1,0:T(8,128)(2,1)} %all-gather.2.cloned.1.call-done, bf16[128,1024]{1,0:T(8,128)(2,1)S(1)} %bitcast.164, bf16[128,1024]{1,0:T(8,128)(2,1)S(1)} %bitcast.163, bf16[1,128,1024]{2,1,0:T(8,128)(2,1)} %param.15), kind=kOutput, calls=%fused_computation.74 | convolution fusion | flops 538312704 | bytes 5242880 | tf_op jit(solution)/shard_map/fc,dc->fd/dot_general | solution.py:178
  146.1 3.0 %reduce.8 = bf16[1024,128]{1,0:T(8,128)(2,1)} reduce(bf16[1024,1,128]{2,1,0:T(2,128)(2,1)S(1)} %bitcast.180, bf16[]{:T(256)} %broadcast.119), dimensions={1}, to_apply=%bitcast.135.reduce_sub_computation | reduce | bytes 524290
  149.0 1.7 reshape.219
  150.7 4.3 %all-to-all-start.4 = ((bf16[4,2,16384]{2,1,0:T(2,128)(2,1)}), bf16[4,2,16384]{2,1,0:T(2,128)(2,1)}, u32[]{:S(2)}, u32[]{:S(2)}) async-start(bf16[4,2,16384]{2,1,0:T(2,128)(2,1)} %reshape.219), calls=%async_computation.4 | async-start | bytes 524288 | tf_op jit(solution)/shard_map/all_to_all | solution.py:185
  155.0 61.4 %all-reduce.3.cloned.1.call-done = f32[31,1024]{1,0:T(8,128)} async-done(((f32[31,1024]{1,0:T(8,128)}), f32[31,1024]{1,0:T(8,128)}) %all-reduce.3.cloned.1.call-update) | async-done | bytes 126992 | tf_op jit(solution)/shard_map/psum | solution.py:161
  216.4 1.6 broadcast_multiply_fusion
  218.0 1.2 reshape.220
  219.5 1.5 convolution_convert_fusion.3
  221.1 3.1 %multiply_convert_fusion = bf16[4,512,512]{1,2,0:T(8,128)(2,1)S(1)} fusion(bf16[512,4,64]{0,2,1:T(8,128)(2,1)S(1)} %reshape_squeeze.18, bf16[512,4,64]{0,2,1:T(8,128)(2,1)S(1)} %copy-done.7, f32[4,512]{1,0:T(4,128)S(1)} %bitcast.288, f32[4,512,512]{1,2,0:T(8,128)} %get-tuple-element.138, f32[4,512]{1,0:T(4,128)S(1)} %copy-done.14), kind=kOutput, calls=%fused_computation.30 | convolution fusion | flops 139460608 | bytes 6832128 | tf_op jit(solution)/shard_map/while/body/eval_jaxpr/qhd,khd->hqk/dot_general | solution.py:69
  224.7 2.3 reduce.11
  227.7 4.0 %all-to-all-start.7 = ((bf16[4,2,16384]{2,1,0:T(2,128)(2,1)}), bf16[4,2,16384]{2,1,0:T(2,128)(2,1)}, u32[]{:S(2)}, u32[]{:S(2)}) async-start(bf16[4,2,16384]{2,1,0:T(2,128)(2,1)} %reshape.225), calls=%async_computation.7 | async-start | bytes 524288 | tf_op jit(solution)/shard_map/all_to_all | solution.py:192
  231.7 1.7 convolution_convert_fusion.4
  233.9 2.3 reduce.10
  237.8 3.4 %all-to-all-start.6 = ((bf16[4,2,16384]{2,1,0:T(2,128)(2,1)}), bf16[4,2,16384]{2,1,0:T(2,128)(2,1)S(1)}, u32[]{:S(2)}, u32[]{:S(2)}) async-start(bf16[4,2,16384]{2,1,0:T(2,128)(2,1)} %reshape.223), calls=%async_computation.6 | async-start | bytes 524288 | tf_op jit(solution)/shard_map/all_to_all | solution.py:191
  241.2 1.4 convolution_convert_fusion.1
  243.1 2.3 reduce.9
  246.1 1.1 all-to-all-done.6
  247.3 3.4 %all-to-all-start.5 = ((bf16[4,2,16384]{2,1,0:T(2,128)(2,1)}), bf16[4,2,16384]{2,1,0:T(2,128)(2,1)S(1)}, u32[]{:S(2)}, u32[]{:S(2)}) async-start(bf16[4,2,16384]{2,1,0:T(2,128)(2,1)} %reshape.221), calls=%async_computation.5 | async-start | bytes 524288 | tf_op jit(solution)/shard_map/all_to_all | solution.py:190
  251.5 1.2 reshape.226
  255.1 1.6 all-to-all-done.5
  (102 shorter events, 25.1 us)
Async XLA Ops:
  7.2 20.1 %copy-start.8 = (bf16[1,128,1024]{2,1,0:T(8,128)(2,1)S(1)}, bf16[1,128,1024]{2,1,0:T(8,128)(2,1)}, u32[]{:S(2)}) copy-start(bf16[1,128,1024]{2,1,0:T(8,128)(2,1)} %param.12) | copy-start | bytes 786436
  7.2 63.6 %all-gather.2.cloned.1.call-start = ((), (), s32[]{:S(2)}) async-start(), calls=%async_computation.8 | async-start | bytes 5242880 | tf_op jit(solution)/shard_map/all_gather | solution.py:125
  7.9 31.9 %copy-start.10 = (bf16[1,128,1024]{2,1,0:T(8,128)(2,1)S(1)}, bf16[1,128,1024]{2,1,0:T(8,128)(2,1)}, u32[]{:S(2)}) copy-start(bf16[1,128,1024]{2,1,0:T(8,128)(2,1)} %param.13) | copy-start | bytes 786436
  12.9 11.0 %all-to-all-start = ((bf16[4,2,16384]{2,1,0:T(2,128)(2,1)}), bf16[4,2,16384]{2,1,0:T(2,128)(2,1)S(1)}, u32[]{:S(2)}, u32[]{:S(2)}) async-start(bf16[4,2,16384]{2,1,0:T(2,128)(2,1)} %reshape.213), calls=%async_computation | async-start | bytes 524288 | tf_op jit(solution)/shard_map/all_to_all | solution.py:108
  23.9 12.5 %all-to-all-start.1 = ((bf16[4,2,16384]{2,1,0:T(2,128)(2,1)}), bf16[4,2,16384]{2,1,0:T(2,128)(2,1)S(1)}, u32[]{:S(2)}, u32[]{:S(2)}) async-start(bf16[4,2,16384]{2,1,0:T(2,128)(2,1)} %reshape.215), calls=%async_computation.1 | async-start | bytes 524288 | tf_op jit(solution)/shard_map/all_to_all | solution.py:109
  36.4 12.5 %all-to-all-start.2 = ((bf16[4,2,16384]{2,1,0:T(2,128)(2,1)}), bf16[4,2,16384]{2,1,0:T(2,128)(2,1)S(1)}, u32[]{:S(2)}, u32[]{:S(2)}) async-start(bf16[4,2,16384]{2,1,0:T(2,128)(2,1)} %reshape.211), calls=%async_computation.2 | async-start | bytes 524288 | tf_op jit(solution)/shard_map/all_to_all | solution.py:110
  41.3 11.8 %copy-start.5 = (bf16[512,4,64]{0,2,1:T(8,128)(2,1)}, bf16[512,4,64]{0,2,1:T(8,128)(2,1)S(1)}, u32[]{:S(2)}) copy-start(bf16[512,4,64]{0,2,1:T(8,128)(2,1)S(1)} %reshape_squeeze.15) | copy-start | bytes 786436
  42.0 11.1 %copy-start.4 = (bf16[512,4,64]{0,2,1:T(8,128)(2,1)}, bf16[512,4,64]{0,2,1:T(8,128)(2,1)S(1)}, u32[]{:S(2)}) copy-start(bf16[512,4,64]{0,2,1:T(8,128)(2,1)S(1)} %reshape_squeeze.16) | copy-start | bytes 786436
  49.6 6.3 %copy-start.6 = (bf16[512,4,64]{0,2,1:T(8,128)(2,1)}, bf16[512,4,64]{0,2,1:T(8,128)(2,1)S(1)}, u32[]{:S(2)}) copy-start(bf16[512,4,64]{0,2,1:T(8,128)(2,1)S(1)} %reshape_squeeze.17) | copy-start | bytes 786436
  53.1 3.3 %copy-start.13 = (f32[4,512]{1,0:T(4,128)}, f32[4,512]{1,0:T(4,128)S(1)}, u32[]{:S(2)}) copy-start(f32[4,512]{1,0:T(4,128)S(1)} %get-tuple-element.137) | copy-start | bytes 24580
  55.9 7.6 %copy-start.11 = (f32[31,1024]{1,0:T(8,128)S(1)}, f32[31,1024]{1,0:T(8,128)}, u32[]{:S(2)}) copy-start(f32[31,1024]{1,0:T(8,128)} %param.16) | copy-start | bytes 380932
  59.8 9.4 %all-to-all-start.3 = ((bf16[4,2,16384]{2,1,0:T(2,128)(2,1)}), bf16[4,2,16384]{2,1,0:T(2,128)(2,1)S(1)}, u32[]{:S(2)}, u32[]{:S(2)}) async-start(bf16[4,2,16384]{2,1,0:T(2,128)(2,1)} %reshape.217), calls=%async_computation.3 | async-start | bytes 524288 | tf_op jit(solution)/shard_map/all_to_all | solution.py:113
  63.4 153.0 %all-reduce.3.cloned.1.call-start = ((), (), s32[]{:S(2)}) async-start(), calls=%async_computation.9 | async-start | bytes 262144 | tf_op jit(solution)/shard_map/psum | solution.py:161
  74.5 5.4 %collective-permute-start = (bf16[1,30,1024]{2,1,0:T(8,128)(2,1)}, bf16[1,30,1024]{2,1,0:T(8,128)(2,1)}, u32[]{:S(2)}, u32[]{:S(2)}) collective-permute-start(bf16[1,30,1024]{2,1,0:T(8,128)(2,1)} %slice.448), channel_id=1, source_target_pairs={{0,1},{1,2},{2,3},{4,5},{5,6},{6,7},{8,9},{9,10},{10,11},{12,13},{... | collective-permute-start | bytes 184328 | tf_op jit(solution)/shard_map/ppermute | solution.py:12
  80.9 3.5 %copy-start.9 = (bf16[1,128,1024]{2,1,0:T(8,128)(2,1)S(1)}, bf16[1,128,1024]{2,1,0:T(8,128)(2,1)}, u32[]{:S(2)}) copy-start(bf16[1,128,1024]{2,1,0:T(8,128)(2,1)} %param.19) | copy-start | bytes 786436
  81.0 3.5 %copy-start.12 = (f32[1024]{0:T(1024)S(1)}, f32[1024]{0:T(1024)}, u32[]{:S(2)}) copy-start(f32[1024]{0:T(1024)} %param.17) | copy-start | bytes 12292
  81.0 3.5 %copy-start.15 = (f32[1024]{0:T(1024)S(1)}, f32[1024]{0:T(1024)}, u32[]{:S(2)}) copy-start(f32[1024]{0:T(1024)} %param.18) | copy-start | bytes 12292
  91.6 46.0 %collective-permute-start.1 = (f32[1,30,1024]{2,1,0:T(8,128)}, f32[1,30,1024]{2,1,0:T(8,128)S(1)}, u32[]{:S(2)}, u32[]{:S(2)}) collective-permute-start(f32[1,30,1024]{2,1,0:T(8,128)} %slice.480), channel_id=1, source_target_pairs={{1,0},{2,1},{3,2},{5,4},{6,5},{7,6},{9,8},{10,9},{11,10},{13,12},{... | collective-permute-start | bytes 368648 | tf_op jit(solution)/shard_map/ppermute | solution.py:12
  141.2 0.7 copy-start
  145.6 73.6 %copy-start.2 = (bf16[1,128,1024]{2,1,0:T(8,128)(2,1)}, bf16[1,128,1024]{2,1,0:T(8,128)(2,1)S(1)}, u32[]{:S(2)}) copy-start(bf16[1,128,1024]{2,1,0:T(8,128)(2,1)S(1)} %fusion.8) | copy-start | bytes 786436
  145.7 75.4 %copy-start.14 = (f32[4,512]{1,0:T(4,128)S(1)}, f32[4,512]{1,0:T(4,128)}, u32[]{:S(2)}) copy-start(f32[4,512]{1,0:T(4,128)} %copy-done.13) | copy-start | bytes 24580
  150.7 67.2 %all-to-all-start.4 = ((bf16[4,2,16384]{2,1,0:T(2,128)(2,1)}), bf16[4,2,16384]{2,1,0:T(2,128)(2,1)}, u32[]{:S(2)}, u32[]{:S(2)}) async-start(bf16[4,2,16384]{2,1,0:T(2,128)(2,1)} %reshape.219), calls=%async_computation.4 | async-start | bytes 524288 | tf_op jit(solution)/shard_map/all_to_all | solution.py:185
  219.2 1.9 copy-start.7
  221.1 3.1 %copy-start.3 = (bf16[4,64,512]{2,1,0:T(8,128)(2,1)S(1)}, bf16[4,64,512]{2,1,0:T(8,128)(2,1)}, u32[]{:S(2)}) copy-start(bf16[4,64,512]{2,1,0:T(8,128)(2,1)} %convolution_convert_fusion.3) | copy-start | bytes 786436
  227.7 10.1 %all-to-all-start.7 = ((bf16[4,2,16384]{2,1,0:T(2,128)(2,1)}), bf16[4,2,16384]{2,1,0:T(2,128)(2,1)}, u32[]{:S(2)}, u32[]{:S(2)}) async-start(bf16[4,2,16384]{2,1,0:T(2,128)(2,1)} %reshape.225), calls=%async_computation.7 | async-start | bytes 524288 | tf_op jit(solution)/shard_map/all_to_all | solution.py:192
  233.4 17.2 %copy-start.1 = (bf16[1,128,1024]{2,1,0:T(8,128)(2,1)S(1)}, bf16[1,128,1024]{2,1,0:T(8,128)(2,1)}, u32[]{:S(2)}) copy-start(bf16[1,128,1024]{2,1,0:T(8,128)(2,1)} %copy-done) | copy-start | bytes 786436
  237.8 9.4 %all-to-all-start.6 = ((bf16[4,2,16384]{2,1,0:T(2,128)(2,1)}), bf16[4,2,16384]{2,1,0:T(2,128)(2,1)S(1)}, u32[]{:S(2)}, u32[]{:S(2)}) async-start(bf16[4,2,16384]{2,1,0:T(2,128)(2,1)} %reshape.223), calls=%async_computation.6 | async-start | bytes 524288 | tf_op jit(solution)/shard_map/all_to_all | solution.py:191
  247.3 9.4 %all-to-all-start.5 = ((bf16[4,2,16384]{2,1,0:T(2,128)(2,1)}), bf16[4,2,16384]{2,1,0:T(2,128)(2,1)S(1)}, u32[]{:S(2)}, u32[]{:S(2)}) async-start(bf16[4,2,16384]{2,1,0:T(2,128)(2,1)} %reshape.221), calls=%async_computation.5 | async-start | bytes 524288 | tf_op jit(solution)/shard_map/all_to_all | solution.py:190
Sparse Core Ops, SparseCore 0:
  9.6 43.2 all-gather.1
  91.7 124.6 all-reduce.2
where the time goes:
time: 266 us; the launch traced here: 265 us
  waiting for transfers between devices  85.9 us (32%)
  blocking collectives  43.4 us (16%)
  other arithmetic  38.5 us (14%)
  starting transfers between devices  33.3 us (13%)
  local copies, waits for them, and re-layouts  30.8 us (12%)
  matrix products  18.3 us (7%)
  between operations  14.8 us (6%)
    psum x1, waiting for transfers between devices, shards(): lax.psum((kernel_term, gain_term, bias_term), ('dp', 'seq'))  61.4 us
    psum x1, blocking collectives, shards(): lax.psum((kernel_term, gain_term, bias_term), ('dp', 'seq'))  43.4 us
    unnamed x65, local copies, waits for them, and re-layouts  20.7 us
    unnamed x8, other arithmetic  18.7 us
    all_to_all x1, waiting for transfers between devices, shards(): lax.all_to_all(value_vecs, 'seq', split_axis=2, concat_axis=1, tiled=True)  6.95 us
    all_to_all x1, waiting for transfers between devices, shards(): lax.all_to_all(key_vecs, 'seq', split_axis=2, concat_axis=1, tiled=True)  5.69 us
  transfers between devices with their start and end apart: 12, of which 8 were waited for; matrix products, arithmetic and copies ran while one was open for 23% of the time, Pallas kernels for 0%

commit v1 on v0

--- a/solution.py
+++ b/solution.py
@@ -1,7 +1,10 @@
+import functools
 import jax
 import jax.numpy as jnp
 from jax import lax
 from jax.sharding import PartitionSpec as P
+from jax.experimental import pallas as pl
+from jax.experimental.pallas import tpu as pltpu
 
 HEADS = 16
 
@@ -205,6 +208,469 @@
     )
 
 
+BF = jnp.bfloat16
+F32 = jnp.float32
+HALO = 32
+LANES = 128
+TERM_ROWS = 40
+
+
+def fused_kernel(
+    dims,
+    q_ref, k_ref, v_ref, res_ref, w_ref, cg_ref, taps_ref, gain_ref, bias_ref, og_ref,
+    ctx_out, conv_out, dq_out, dk_out, dv_out, ig_out, rg_out, kg_out, gg_out, bg_out,
+    q_h, k_h, v_h, g_h, qt, kt, vt, gt, ctxt, ctx_h, prob, ds_s, pb_s, dqt, dq_h, dk_h, dv_h,
+    w_full, mixed, a_s, sig_s, glu_f, dw, ng_s, dg, part, rs_buf, s2_buf, fin,
+    ssem, rsem, lsem,
+):
+    n_seq, n_dp, rows, channels, taps, depth = dims
+    own = channels // n_seq
+    pairs = own // LANES
+    frames = rows * n_seq
+    chunks = channels // LANES
+    scaling = depth ** (-0.5)
+    me = lax.axis_index("seq")
+    dp = lax.axis_index("dp")
+    core = lax.rem(me, 2)
+    mate = me + 1 - 2 * core
+    across = lax.rem(me + 2, n_seq)
+    x_pos = lax.rem(dp, 2)
+    x_dp = dp + 1 - 2 * x_pos
+    counter = [0]
+
+    def remote(src, dst, device):
+        index = counter[0]
+        counter[0] += 1
+        return pltpu.make_async_remote_copy(
+            src_ref=src, dst_ref=dst, send_sem=ssem.at[index], recv_sem=rsem.at[index],
+            device_id=device, device_id_type=pl.DeviceIdType.MESH,
+        )
+
+    peers = [lax.rem(me + d, n_seq) for d in range(1, n_seq)]
+    dp_peers = [lax.rem(dp + d, n_dp) for d in range(1, n_dp)]
+    barrier = pltpu.get_barrier_semaphore()
+    for p in peers:
+        pl.semaphore_signal(barrier, inc=1, device_id=(dp, p), device_id_type=pl.DeviceIdType.MESH)
+    for p in dp_peers:
+        pl.semaphore_signal(barrier, inc=1, device_id=(p, me), device_id_type=pl.DeviceIdType.MESH)
+    pl.semaphore_wait(barrier, n_seq - 1 + n_dp - 1)
+
+    pending = []
+
+    def at(value, size):
+        return pl.ds(pl.multiple_of(value * size, size), size)
+
+    def scatter_heads(src, dst):
+        copies = []
+        for p in peers:
+            copy = remote(src.at[:, at(p, own)], dst.at[at(me, rows), :], (dp, p))
+            copy.start()
+            copies.append(copy)
+        return copies
+
+    sends = []
+    local = []
+    for t, (src, dst) in enumerate(((q_ref, q_h), (k_ref, k_h), (v_ref, v_h))):
+        sends.append(scatter_heads(src, dst))
+        copy = pltpu.make_async_copy(src.at[:, at(me, own)], dst.at[at(me, rows), :], lsem.at[t])
+        copy.start()
+        local.append(copy)
+
+    w_rows = w_ref.shape[0]
+    half = w_rows // 2
+    pieces = 2
+    piece = half // pieces
+    w_mate = remote(w_ref, w_full.at[at(me, w_rows), :], (dp, mate))
+    w_mate.start()
+    w_self = pltpu.make_async_copy(w_ref, w_full.at[at(me, w_rows), :], lsem.at[3])
+    w_self.start()
+    w_across = []
+    for j in range(pieces):
+        start = pl.multiple_of(x_pos * half + j * piece, piece)
+        copy = remote(
+            w_ref.at[pl.ds(start, piece), :],
+            w_full.at[pl.ds(pl.multiple_of(me * w_rows + start, piece), piece), :],
+            (dp, across),
+        )
+        copy.start()
+        w_across.append(copy)
+
+    def flip(ref):
+        return ref[...].astype(F32).T
+
+    def arrive(t):
+        local[t].wait()
+        for copy in sends[t]:
+            copy.wait_recv()
+
+    arrive(0)
+    qt[...] = (flip(q_h) * scaling).astype(BF)
+    arrive(1)
+    kt[...] = flip(k_h).astype(BF)
+    arrive(2)
+    vt[...] = flip(v_h).astype(BF)
+
+    q_block = min(256, frames)
+
+    def forward_head(h):
+        hr = slice(h * depth, (h + 1) * depth)
+
+        def body(b, carry):
+            cols = at(b, q_block)
+            scores = jnp.dot(k_h[:, hr], qt[hr, cols], preferred_element_type=F32)
+            shifted = jnp.exp(scores - jnp.max(scores, axis=0, keepdims=True))
+            p = shifted * (1.0 / jnp.sum(shifted, axis=0, keepdims=True))
+            prob[h, :, cols] = p
+            ctxt[hr, cols] = jnp.dot(vt[hr, :], p.astype(BF), preferred_element_type=F32).astype(BF)
+            return carry
+
+        lax.fori_loop(0, frames // q_block, body, 0)
+
+    def gather_pair(src, dst, pair, t):
+        copies = []
+        width = LANES
+        target = pl.ds(pl.multiple_of(me * own + pair * width, width), width)
+        source = slice(pair * width, (pair + 1) * width)
+        for p in peers:
+            copy = remote(src.at[at(p, rows), source], dst.at[:, target], (dp, p))
+            copy.start()
+            copies.append(copy)
+        keep = pltpu.make_async_copy(src.at[at(me, rows), source], dst.at[:, target], lsem.at[t])
+        keep.start()
+        return copies, keep
+
+    ctx_copies = []
+    for pair in range(pairs):
+        forward_head(2 * pair)
+        forward_head(2 * pair + 1)
+        pc = slice(pair * LANES, (pair + 1) * LANES)
+        ctx_h[:, pc] = ctxt[pc, :].astype(F32).T.astype(BF)
+        ctx_copies.append(gather_pair(ctx_h, ctx_out, pair, 4 + pair))
+
+    w_x, w_fwd1, w_fwd2 = [], [], []
+    for j in range(pieces):
+        w_across[j].wait_recv()
+        here = pl.ds(pl.multiple_of(across * w_rows + x_pos * half + j * piece, piece), piece)
+        copy = remote(w_full.at[here, :], w_full.at[here, :], (x_dp, me))
+        copy.start()
+        w_x.append(copy)
+        copy = remote(w_full.at[here, :], w_full.at[here, :], (dp, mate))
+        copy.start()
+        w_fwd1.append(copy)
+    for j in range(pieces):
+        w_x[j].wait_recv()
+        here = pl.ds(
+            pl.multiple_of(across * w_rows + (1 - x_pos) * half + j * piece, piece), piece
+        )
+        copy = remote(w_full.at[here, :], w_full.at[here, :], (dp, mate))
+        copy.start()
+        w_fwd2.append(copy)
+
+    for copies, keep in ctx_copies:
+        keep.wait()
+        for copy in copies:
+            copy.wait_recv()
+    mixed[...] = (res_ref[...].astype(F32) + ctx_out[...].astype(F32)).astype(BF)
+    w_self.wait()
+    w_mate.wait_recv()
+    for copy in w_fwd1 + w_fwd2:
+        copy.wait_recv()
+
+    wide = 2 * LANES
+
+    def conv_in(i, carry):
+        cols = at(i, wide)
+        gates = pl.ds(pl.multiple_of(channels + i * wide, wide), wide)
+        a = jnp.dot(mixed[...], w_full[:, cols], preferred_element_type=F32).astype(BF)
+        b = jnp.dot(mixed[...], w_full[:, gates], preferred_element_type=F32).astype(BF)
+        sig = jax.nn.sigmoid(b.astype(F32))
+        a_s[:, cols] = a
+        sig_s[:, cols] = sig
+        glu = (a.astype(F32) * sig).astype(BF).astype(F32)
+        glu_f[2 * i, HALO : HALO + rows, :] = glu[:, :LANES]
+        glu_f[2 * i + 1, HALO : HALO + rows, :] = glu[:, LANES:]
+        return carry
+
+    lax.fori_loop(0, channels // wide, conv_in, 0)
+    halo1 = remote(
+        glu_f.at[:, rows : rows + HALO, :], glu_f.at[:, 0:HALO, :], (dp, lax.rem(me + 1, n_seq))
+    )
+    halo1.start()
+    halo1.wait_recv()
+    halo1.wait_send()
+
+    @pl.when(me == 0)
+    def _():
+        glu_f[:, 0:HALO, :] = jnp.zeros((chunks, HALO, LANES), F32)
+
+    span = taps - 1
+    base = HALO - span
+
+    def depth_conv(c, total):
+        lanes = at(c, LANES)
+        acc = jnp.zeros((rows, LANES), F32)
+        for o in range(taps):
+            acc = acc + taps_ref[o : o + 1, lanes] * glu_f[c, base + o : base + o + rows, :]
+        dw[c] = acc
+        return total + acc
+
+    zero = jnp.zeros((rows, LANES), F32)
+    total = lax.fori_loop(0, chunks, depth_conv, zero)
+    average = jnp.sum(total, axis=1, keepdims=True) * (1.0 / channels)
+
+    def squares(c, total):
+        centered = dw[c] - average
+        return total + centered * centered
+
+    total = lax.fori_loop(0, chunks, squares, zero)
+    variance = jnp.sum(total, axis=1, keepdims=True) * (1.0 / channels)
+    inverse = lax.rsqrt(variance + 1e-05)
+
+    def norm_step(c, carry):
+        s1, s2 = carry
+        lanes = at(c, LANES)
+        normed = (dw[c] - average) * inverse
+        affine = normed * gain_ref[:, lanes] + bias_ref[:, lanes]
+        sig = jax.nn.sigmoid(affine)
+        conv_out[:, lanes] = (affine * sig).astype(BF)
+        affine_grad = og_ref[:, lanes].astype(F32) * (sig * (1.0 + affine * (1.0 - sig)))
+        part[c, taps : taps + 1, :] = jnp.sum(affine_grad * normed, axis=0, keepdims=True)
+        part[c, taps + 1 : taps + 2, :] = jnp.sum(affine_grad, axis=0, keepdims=True)
+        normed_grad = affine_grad * gain_ref[:, lanes]
+        dw[c] = normed
+        ng_s[c] = normed_grad
+        return s1 + normed_grad, s2 + normed_grad * normed
+
+    s1, s2 = lax.fori_loop(0, chunks, norm_step, (zero, zero))
+    m1 = jnp.sum(s1, axis=1, keepdims=True) * (1.0 / channels)
+    m2 = jnp.sum(s2, axis=1, keepdims=True) * (1.0 / channels)
+
+    def depth_grad_step(c, carry):
+        dg[c, 0:rows, :] = inverse * (ng_s[c] - m1 - dw[c] * m2)
+        return carry
+
+    lax.fori_loop(0, chunks, depth_grad_step, 0)
+    halo2 = remote(
+        dg.at[:, 0:HALO, :], dg.at[:, rows : rows + HALO, :], (dp, lax.rem(me + n_seq - 1, n_seq))
+    )
+    halo2.start()
+
+    def tap_grad(c, carry):
+        grad = dg[c, 0:rows, :]
+        for o in range(taps):
+            part[c, o : o + 1, :] = jnp.sum(
+                grad * glu_f[c, base + o : base + o + rows, :], axis=0, keepdims=True
+            )
+        part[c, taps + 2 : TERM_ROWS, :] = jnp.zeros((TERM_ROWS - taps - 2, LANES), F32)
+        return carry
+
+    lax.fori_loop(0, chunks, tap_grad, 0)
+    reduce1 = []
+    for d, p in enumerate(dp_peers):
+        copy = remote(part.at[p], rs_buf.at[d], (p, me))
+        copy.start()
+        reduce1.append(copy)
+
+    halo2.wait_recv()
+    halo2.wait_send()
+
+    @pl.when(me == n_seq - 1)
+    def _():
+        dg[:, rows : rows + HALO, :] = jnp.zeros((chunks, HALO, LANES), F32)
+
+    def glu_back(c, carry):
+        lanes = at(c, LANES)
+        gates = pl.ds(pl.multiple_of(channels + c * LANES, LANES), LANES)
+        acc = jnp.zeros((rows, LANES), F32)
+        for o in range(taps):
+            acc = acc + taps_ref[o : o + 1, lanes] * dg[c, span - o : span - o + rows, :]
+        sig = sig_s[:, lanes]
+        ig_out[:, lanes] = (acc * sig).astype(BF)
+        ig_out[:, gates] = (acc * a_s[:, lanes].astype(F32) * sig * (1.0 - sig)).astype(BF)
+        return carry
+
+    lax.fori_loop(0, chunks, glu_back, 0)
+
+    def mixed_back(i, carry):
+        cols = at(i, wide)
+        grad = lax.dot_general(
+            ig_out[...], w_full[cols, :], (((1,), (1,)), ((), ())), preferred_element_type=F32
+        )
+        rg_out[:, cols] = (cg_ref[:, cols].astype(F32) + grad).astype(BF)
+        return carry
+
+    lax.fori_loop(0, channels // wide, mixed_back, 0)
+    g_send = scatter_heads(rg_out, g_h)
+    g_self = pltpu.make_async_copy(
+        rg_out.at[:, at(me, own)], g_h.at[at(me, rows), :], lsem.at[6]
+    )
+    g_self.start()
+
+    for copy in reduce1:
+        copy.wait_recv()
+    total = part[dp]
+    for d in range(n_dp - 1):
+        total = total + rs_buf[d]
+    s2_buf[me] = total
+    reduce2 = []
+    for p in peers:
+        copy = remote(s2_buf.at[me], s2_buf.at[me], (dp, p))
+        copy.start()
+        reduce2.append(copy)
+
+    g_self.wait()
+    for copy in g_send:
+        copy.wait_recv()
+    gt[...] = flip(g_h).astype(BF)
+
+    def backward_head(h):
+        hr = slice(h * depth, (h + 1) * depth)
+        slot = h % 2
+
+        def body(b, carry):
+            cols = at(b, q_block)
+            grad = gt[hr, cols]
+            dots = jnp.sum(
+                grad.astype(F32) * ctxt[hr, cols].astype(F32), axis=0, keepdims=True
+            )
+            prob_grad = jnp.dot(v_h[:, hr], grad, preferred_element_type=F32)
+            p = prob[h, :, cols]
+            score_grad = (p * (prob_grad - dots) * scaling).astype(BF)
+            pb_s[slot, :, cols] = p.astype(BF)
+            ds_s[slot, :, cols] = score_grad
+            dqt[hr, cols] = jnp.dot(kt[hr, :], score_grad, preferred_element_type=F32)
+            return carry
+
+        lax.fori_loop(0, frames // q_block, body, 0)
+
+    first = lax.broadcasted_iota(jnp.int32, (frames, LANES), 1) < depth
+    out_copies = []
+    reduce3 = []
+    for pair in range(pairs):
+        pc = slice(pair * LANES, (pair + 1) * LANES)
+        backward_head(2 * pair)
+        backward_head(2 * pair + 1)
+        dq_h[:, pc] = dqt[pc, :].T.astype(BF)
+        out_copies.append(gather_pair(dq_h, dq_out, pair, 7 + 3 * pair))
+        left = jnp.dot(ds_s[0], q_h[:, pc], preferred_element_type=F32)
+        right = jnp.dot(ds_s[1], q_h[:, pc], preferred_element_type=F32)
+        dk_h[:, pc] = jnp.where(first, left, right).astype(BF)
+        out_copies.append(gather_pair(dk_h, dk_out, pair, 8 + 3 * pair))
+        left = jnp.dot(pb_s[0], g_h[:, pc], preferred_element_type=F32)
+        right = jnp.dot(pb_s[1], g_h[:, pc], preferred_element_type=F32)
+        dv_h[:, pc] = jnp.where(first, left, right).astype(BF)
+        out_copies.append(gather_pair(dv_h, dv_out, pair, 9 + 3 * pair))
+        if pair == 0:
+            for copy in reduce2:
+                copy.wait_recv()
+            total = s2_buf[0]
+            for s in range(1, n_seq):
+                total = total + s2_buf[s]
+            fin[dp] = total * (1.0 / n_dp)
+            for p in dp_peers:
+                copy = remote(fin.at[dp], fin.at[dp], (p, me))
+                copy.start()
+                reduce3.append(copy)
+
+    for copy in reduce3:
+        copy.wait_recv()
+    for c in range(chunks):
+        lanes = slice(c * LANES, (c + 1) * LANES)
+        kg_out[:, lanes] = fin[c, 0:taps, :]
+        gg_out[:, lanes] = fin[c, taps : taps + 1, :]
+        bg_out[:, lanes] = fin[c, taps + 1 : taps + 2, :]
+
+    for copies, keep in out_copies:
+        keep.wait()
+        for copy in copies:
+            copy.wait_recv()
+    for copies in sends + [c for c, _ in ctx_copies] + [c for c, _ in out_copies]:
+        for copy in copies:
+            copy.wait_send()
+    for copy in (
+        [w_mate] + w_across + w_x + w_fwd1 + w_fwd2 + g_send + reduce1 + reduce2 + reduce3
+    ):
+        copy.wait_send()
+
+
+def fused_shards(
+    queries, key_vecs, value_vecs, residual_in, point_weight, context_grad, depth_kernel,
+    norm_gain, norm_bias, conv_grad,
+):
+    n_seq = lax.axis_size("seq")
+    n_dp = lax.axis_size("dp")
+    rows, channels = queries.shape[1:]
+    taps = depth_kernel.shape[0]
+    depth = channels // HEADS
+    frames = rows * n_seq
+    own = channels // n_seq
+    heads = own // depth
+    chunks = channels // LANES
+    s = jax.ShapeDtypeStruct
+    vm = pltpu.VMEM
+    block = s((rows, channels), BF)
+    head_rows = vm((frames, own), BF)
+    head_cols = vm((own, frames), BF)
+    n_copies = 96
+    scratch = (
+        [head_rows] * 4 + [head_cols] * 5 + [head_rows]
+        + [vm((heads, frames, frames), F32), vm((2, frames, frames), BF), vm((2, frames, frames), BF)]
+        + [vm((own, frames), F32)] + [head_rows] * 3
+        + [
+            vm((channels, 2 * channels), BF),
+            vm((rows, channels), BF),
+            vm((rows, channels), BF),
+            vm((rows, channels), F32),
+            vm((chunks, HALO + rows, LANES), F32),
+            vm((chunks, rows, LANES), F32),
+            vm((chunks, rows, LANES), F32),
+            vm((chunks, rows + HALO, LANES), F32),
+            vm((chunks, TERM_ROWS, LANES), F32),
+            vm((n_dp - 1, TERM_ROWS, LANES), F32),
+            vm((n_seq, TERM_ROWS, LANES), F32),
+            vm((chunks, TERM_ROWS, LANES), F32),
+            pltpu.SemaphoreType.DMA((n_copies,)),
+            pltpu.SemaphoreType.DMA((n_copies,)),
+            pltpu.SemaphoreType.DMA((16,)),
+        ]
+    )
+    spec = pl.BlockSpec(memory_space=pltpu.VMEM)
+    outs = pl.pallas_call(
+        functools.partial(fused_kernel, (n_seq, n_dp, rows, channels, taps, depth)),
+        out_shape=(
+            block, block, block, block, block, s((rows, 2 * channels), BF), block,
+            s((taps, channels), F32), s((1, channels), F32), s((1, channels), F32),
+        ),
+        in_specs=[spec] * 10,
+        out_specs=(spec,) * 10,
+        scratch_shapes=scratch,
+        compiler_params=pltpu.CompilerParams(
+            collective_id=0, has_side_effects=True, vmem_limit_bytes=56 * 1024 * 1024
+        ),
+    )(
+        queries[0], key_vecs[0], value_vecs[0], residual_in[0], point_weight, context_grad[0],
+        depth_kernel, norm_gain[None], norm_bias[None], conv_grad[0],
+    )
+    return tuple(o[None] for o in outs[:7]) + (outs[7], outs[8][0], outs[9][0])
+
+
+def chosen(*args):
+    n_seq = lax.axis_size("seq")
+    n_dp = lax.axis_size("dp")
+    recs, rows, channels = args[0].shape
+    fits = (
+        n_seq == 4
+        and recs == 1
+        and rows % 128 == 0
+        and channels % (LANES * n_seq) == 0
+        and 2 * channels == LANES * HEADS
+        and channels // LANES == n_dp
+        and rows * n_seq <= 512
+        and args[6].shape[0] <= 32
+    )
+    return fused_shards(*args) if fits else shards(*args)
+
+
 def solution(mesh):
     in_specs = (
         P("dp", "seq", None),
@@ -230,4 +696,4 @@
         P(),
         P(),
     )
-    return jax.shard_map(shards, mesh=mesh, in_specs=in_specs, out_specs=out_specs, check_vma=False)
+    return jax.shard_map(chosen, mesh=mesh, in_specs=in_specs, out_specs=out_specs, check_vma=False)

time: 266 us -> 82 us (0.31)
  waiting for transfers between devices: 85.9 us -> 0 us
  Pallas kernels: 0 us -> 71.8 us
  blocking collectives: 43.4 us -> 0 us
  other arithmetic: 38.5 us -> 0 us
  starting transfers between devices: 33.3 us -> 0 us
  local copies, waits for them, and re-layouts: 30.8 us -> 9.23 us
  matrix products: 18.3 us -> 0 us
  between operations: 14.8 us -> 0.68 us
    pallas_call x0 -> x1, Pallas kernels: none -> 71.8 us  [fused_shards(): pl.pallas_call(functools.partial(fused_kernel, (n_seq, n_dp, rows, channe...]
    psum x1 -> x0, waiting for transfers between devices: 61.4 us -> none  [shards(): lax.psum((kernel_term, gain_term, bias_term), ('dp', 'seq'))]
    psum x1 -> x0, blocking collectives: 43.4 us -> none  [shards(): lax.psum((kernel_term, gain_term, bias_term), ('dp', 'seq'))]
    all_to_all x8 -> x0, starting transfers between devices: 29.8 us -> none  [the longest x1 4.26 us: shards(): lax.all_to_all(residual_grad, 'seq', split_axis=2, concat_axis=1, tiled=T...]
    all_to_all x8 -> x0, waiting for transfers between devices: 23.7 us -> none  [the longest x1 6.95 us: shards(): lax.all_to_all(value_vecs, 'seq', split_axis=2, concat_axis=1, tiled=True)]
    unnamed x8 -> x0, other arithmetic: 18.7 us -> none
    dot_general x7 -> x0, matrix products: 14.8 us -> none  [the longest x1 3.74 us: shards(): jnp.einsum('fc,dc->fd', slope_rows, lax.all_gather(point_weight, 'seq', a...]
    unnamed x65 -> x28, local copies, waits for them, and re-layouts: 20.7 us -> 9.23 us
  transfers between devices with their start and end apart: 12 -> 0, of which waited for: 8 -> 0; matrix products, arithmetic and copies ran while one was open for 23% -> 0% of each run, Pallas kernels for 0% -> 0%
where the time goes in v1:
time: 82 us; the launch traced here: 81.7 us
  Pallas kernels  71.8 us (88%)
  local copies, waits for them, and re-layouts  9.23 us (11%)
    pallas_call x1, Pallas kernels, fused_shards(): pl.pallas_call(functools.partial(fused_kernel, (n_seq, n_dp, rows, channe...  71.8 us
    unnamed x28, local copies, waits for them, and re-layouts  9.23 us

profile of v1, /device:TPU:0, one launch (start us, length us, event | category | flops | bytes accessed | tf_op | source)
XLA Modules:
  0.0 81.7 jit_solution(6562627271581535617)
XLA Ops:
  0.6 71.8 %shard_map.177 = (bf16[128,1024]{1,0:T(8,128)(2,1)}, bf16[128,1024]{1,0:T(8,128)(2,1)}, bf16[128,1024]{1,0:T(8,128)(2,1)}, bf16[128,1024]{1,0:T(8,128)(2,1)}, bf...) custom-call(bf16[128,1024]{1,0:T(8,128)(2,1)} %bitcast.24, ...), custom_call_target="tpu_custom_call" | custom-call | tf_op jit(solution)/shard_map/pallas_call | solution.py:638
  72.4 0.0 copy-start.5
  72.4 1.7 %copy.30 = bf16[1,128,1024]{2,1,0:T(8,128)(2,1)} copy(bf16[1,128,1024]{2,1,0:T(8,128)(2,1)} %bitcast.23) | data formatting | bytes 524288
  74.1 0.0 copy-done.5
  74.1 0.0 copy-start.4
  74.1 0.7 copy.31
  74.8 0.3 copy-done.4
  75.2 0.0 copy-start.3
  75.2 0.0 copy-start.2
  75.2 0.7 copy.32
  75.9 0.3 copy-done.3
  76.2 0.0 copy-start
  76.2 0.7 copy.33
  76.9 0.0 copy-done.2
  76.9 0.7 copy.34
  77.6 0.0 copy-done
  77.6 0.0 copy-start.1
  77.6 0.8 copy.35
  78.4 0.3 copy-done.1
  78.7 0.0 copy-start.6
  78.7 0.7 copy.36
  79.4 0.3 copy-done.6
  79.7 0.0 copy-start.8
  79.7 0.7 copy.37
  80.4 0.0 copy-done.8
  80.4 0.0 copy-start.7
  80.4 0.6 copy.38
  81.0 0.1 copy-done.7
  81.1 0.6 copy.39
Async XLA Ops:
  72.4 1.7 %copy-start.5 = (bf16[128,1024]{1,0:T(8,128)(2,1)S(1)}, bf16[128,1024]{1,0:T(8,128)(2,1)}, u32[]{:S(2)}) copy-start(bf16[128,1024]{1,0:T(8,128)(2,1)} %get-tuple-element.21) | copy-start | bytes 786436
  74.1 1.0 %copy-start.4 = (bf16[128,1024]{1,0:T(8,128)(2,1)S(1)}, bf16[128,1024]{1,0:T(8,128)(2,1)}, u32[]{:S(2)}) copy-start(bf16[128,1024]{1,0:T(8,128)(2,1)} %get-tuple-element.22) | copy-start | bytes 786436
  75.2 1.0 %copy-start.3 = (bf16[128,1024]{1,0:T(8,128)(2,1)S(1)}, bf16[128,1024]{1,0:T(8,128)(2,1)}, u32[]{:S(2)}) copy-start(bf16[128,1024]{1,0:T(8,128)(2,1)} %get-tuple-element.23) | copy-start | bytes 786436
  75.2 1.7 %copy-start.2 = (bf16[128,1024]{1,0:T(8,128)(2,1)S(1)}, bf16[128,1024]{1,0:T(8,128)(2,1)}, u32[]{:S(2)}) copy-start(bf16[128,1024]{1,0:T(8,128)(2,1)} %get-tuple-element.24) | copy-start | bytes 786436
  76.2 1.4 %copy-start = (bf16[128,2048]{1,0:T(8,128)(2,1)S(1)}, bf16[128,2048]{1,0:T(8,128)(2,1)}, u32[]{:S(2)}) copy-start(bf16[128,2048]{1,0:T(8,128)(2,1)} %get-tuple-element.25) | copy-start | bytes 1572868
  77.6 1.1 %copy-start.1 = (bf16[128,1024]{1,0:T(8,128)(2,1)S(1)}, bf16[128,1024]{1,0:T(8,128)(2,1)}, u32[]{:S(2)}) copy-start(bf16[128,1024]{1,0:T(8,128)(2,1)} %get-tuple-element.26) | copy-start | bytes 786436
  78.7 1.0 %copy-start.6 = (f32[31,1024]{1,0:T(8,128)S(1)}, f32[31,1024]{1,0:T(8,128)}, u32[]{:S(2)}) copy-start(f32[31,1024]{1,0:T(8,128)} %get-tuple-element.47) | copy-start | bytes 380932
  79.7 0.7 copy-start.8
  80.4 0.7 copy-start.7

commit v2 on v1

--- a/solution.py
+++ b/solution.py
@@ -219,8 +219,8 @@
     dims,
     q_ref, k_ref, v_ref, res_ref, w_ref, cg_ref, taps_ref, gain_ref, bias_ref, og_ref,
     ctx_out, conv_out, dq_out, dk_out, dv_out, ig_out, rg_out, kg_out, gg_out, bg_out,
-    q_h, k_h, v_h, g_h, qt, kt, vt, gt, ctxt, ctx_h, prob, ds_s, pb_s, dqt, dq_h, dk_h, dv_h,
-    w_full, mixed, a_s, sig_s, glu_f, dw, ng_s, dg, part, rs_buf, s2_buf, fin,
+    q_h, k_h, v_h, g_h, qt, kt, vt, gt, ctxt, ctx_h, prob, pb_s, ds_s, dqt, dq_h, dk_h, dv_h,
+    res_v, cg_v, og_v, w_full, pre, mixed, a_s, sig_s, glu_f, dw, ng_s, dg, part, rs_buf, s2_buf, fin,
     ssem, rsem, lsem,
 ):
     n_seq, n_dp, rows, channels, taps, depth = dims
@@ -246,7 +246,9 @@
             device_id=device, device_id_type=pl.DeviceIdType.MESH,
         )
 
-    peers = [lax.rem(me + d, n_seq) for d in range(1, n_seq)]
+    diag = lax.rem(mate + 2, n_seq)
+    chip = lax.div(me, 2)
+    peers = [across, diag, mate]
     dp_peers = [lax.rem(dp + d, n_dp) for d in range(1, n_dp)]
     barrier = pltpu.get_barrier_semaphore()
     for p in peers:
@@ -255,26 +257,32 @@
         pl.semaphore_signal(barrier, inc=1, device_id=(p, me), device_id_type=pl.DeviceIdType.MESH)
     pl.semaphore_wait(barrier, n_seq - 1 + n_dp - 1)
 
-    pending = []
-
     def at(value, size):
         return pl.ds(pl.multiple_of(value * size, size), size)
 
-    def scatter_heads(src, dst):
-        copies = []
-        for p in peers:
-            copy = remote(src.at[:, at(p, own)], dst.at[at(me, rows), :], (dp, p))
-            copy.start()
-            copies.append(copy)
-        return copies
+    loads = []
+    for t, (src, dst) in enumerate(((res_ref, res_v), (cg_ref, cg_v), (og_ref, og_v))):
+        copy = pltpu.make_async_copy(src, dst, lsem.at[t])
+        copy.start()
+        loads.append(copy)
+
+    def head_cols(owner, pair):
+        return pl.ds(pl.multiple_of(owner * own + pair * LANES, LANES), LANES)
 
     sends = []
-    local = []
-    for t, (src, dst) in enumerate(((q_ref, q_h), (k_ref, k_h), (v_ref, v_h))):
-        sends.append(scatter_heads(src, dst))
-        copy = pltpu.make_async_copy(src.at[:, at(me, own)], dst.at[at(me, rows), :], lsem.at[t])
-        copy.start()
-        local.append(copy)
+    for pair in range(pairs):
+        pc = slice(pair * LANES, (pair + 1) * LANES)
+        for t, (src, dst) in enumerate(((q_ref, q_h), (k_ref, k_h), (v_ref, v_h))):
+            copies = []
+            for p in peers:
+                copy = remote(src.at[:, head_cols(p, pair)], dst.at[at(me, rows), pc], (dp, p))
+                copy.start()
+                copies.append(copy)
+            keep = pltpu.make_async_copy(
+                src.at[:, head_cols(me, pair)], dst.at[at(me, rows), pc], lsem.at[4 + 3 * pair + t]
+            )
+            keep.start()
+            sends.append((copies, keep))
 
     w_rows = w_ref.shape[0]
     half = w_rows // 2
@@ -295,20 +303,14 @@
         copy.start()
         w_across.append(copy)
 
-    def flip(ref):
-        return ref[...].astype(F32).T
-
-    def arrive(t):
-        local[t].wait()
-        for copy in sends[t]:
+    def flip(value):
+        return value.astype(F32).T
+
+    def arrive(index):
+        copies, keep = sends[index]
+        keep.wait()
+        for copy in copies:
             copy.wait_recv()
-
-    arrive(0)
-    qt[...] = (flip(q_h) * scaling).astype(BF)
-    arrive(1)
-    kt[...] = flip(k_h).astype(BF)
-    arrive(2)
-    vt[...] = flip(v_h).astype(BF)
 
     q_block = min(256, frames)
 
@@ -320,69 +322,93 @@
             scores = jnp.dot(k_h[:, hr], qt[hr, cols], preferred_element_type=F32)
             shifted = jnp.exp(scores - jnp.max(scores, axis=0, keepdims=True))
             p = shifted * (1.0 / jnp.sum(shifted, axis=0, keepdims=True))
+            rounded = p.astype(BF)
             prob[h, :, cols] = p
-            ctxt[hr, cols] = jnp.dot(vt[hr, :], p.astype(BF), preferred_element_type=F32).astype(BF)
+            pb_s[h, :, cols] = rounded
+            ctxt[hr, cols] = jnp.dot(vt[hr, :], rounded, preferred_element_type=F32).astype(BF)
             return carry
 
         lax.fori_loop(0, frames // q_block, body, 0)
 
     def gather_pair(src, dst, pair, t):
         copies = []
-        width = LANES
-        target = pl.ds(pl.multiple_of(me * own + pair * width, width), width)
-        source = slice(pair * width, (pair + 1) * width)
+        source = slice(pair * LANES, (pair + 1) * LANES)
         for p in peers:
-            copy = remote(src.at[at(p, rows), source], dst.at[:, target], (dp, p))
+            copy = remote(src.at[at(p, rows), source], dst.at[:, head_cols(me, pair)], (dp, p))
             copy.start()
             copies.append(copy)
-        keep = pltpu.make_async_copy(src.at[at(me, rows), source], dst.at[:, target], lsem.at[t])
+        keep = pltpu.make_async_copy(
+            src.at[at(me, rows), source], dst.at[:, head_cols(me, pair)], lsem.at[t]
+        )
         keep.start()
         return copies, keep
 
     ctx_copies = []
     for pair in range(pairs):
+        pc = slice(pair * LANES, (pair + 1) * LANES)
+        arrive(3 * pair)
+        qt[pc, :] = (flip(q_h[:, pc]) * scaling).astype(BF)
+        arrive(3 * pair + 1)
+        arrive(3 * pair + 2)
+        vt[pc, :] = flip(v_h[:, pc]).astype(BF)
         forward_head(2 * pair)
         forward_head(2 * pair + 1)
-        pc = slice(pair * LANES, (pair + 1) * LANES)
-        ctx_h[:, pc] = ctxt[pc, :].astype(F32).T.astype(BF)
-        ctx_copies.append(gather_pair(ctx_h, ctx_out, pair, 4 + pair))
-
-    w_x, w_fwd1, w_fwd2 = [], [], []
+        ctx_h[:, pc] = flip(ctxt[pc, :]).astype(BF)
+        ctx_copies.append(gather_pair(ctx_h, ctx_out, pair, 10 + pair))
+
+    def w_part(owner, side, j):
+        return pl.ds(pl.multiple_of(owner * w_rows + side * half + j * piece, piece), piece)
+
+    def forward(here, device):
+        copy = remote(w_full.at[here, :], w_full.at[here, :], device)
+        copy.start()
+        return copy
+
+    w_x, w_fwd = [], []
     for j in range(pieces):
         w_across[j].wait_recv()
-        here = pl.ds(pl.multiple_of(across * w_rows + x_pos * half + j * piece, piece), piece)
-        copy = remote(w_full.at[here, :], w_full.at[here, :], (x_dp, me))
-        copy.start()
-        w_x.append(copy)
-        copy = remote(w_full.at[here, :], w_full.at[here, :], (dp, mate))
-        copy.start()
-        w_fwd1.append(copy)
+        here = w_part(across, x_pos, j)
+        w_x.append(forward(here, (x_dp, me)))
+        w_fwd.append(forward(here, (dp, mate)))
+        if j == 0:
+            for pair in range(pairs):
+                pc = slice(pair * LANES, (pair + 1) * LANES)
+                kt[pc, :] = flip(k_h[:, pc]).astype(BF)
+
+    for copies, keep in ctx_copies:
+        keep.wait()
+        copies[2].wait_recv()
+    loads[0].wait()
+    w_self.wait()
+    w_mate.wait_recv()
+    near = at(chip, 2 * own)
+    far = at(1 - chip, 2 * own)
+    wide = 2 * LANES
+    mixed[:, near] = (res_v[:, near].astype(F32) + ctx_out[:, near].astype(F32)).astype(BF)
+
+    def conv_near(i, carry):
+        cols = at(i, wide)
+        pre[:, cols] = jnp.dot(mixed[:, near], w_full[near, cols], preferred_element_type=F32)
+        return carry
+
+    lax.fori_loop(0, 2 * channels // wide, conv_near, 0)
     for j in range(pieces):
         w_x[j].wait_recv()
-        here = pl.ds(
-            pl.multiple_of(across * w_rows + (1 - x_pos) * half + j * piece, piece), piece
-        )
-        copy = remote(w_full.at[here, :], w_full.at[here, :], (dp, mate))
-        copy.start()
-        w_fwd2.append(copy)
-
+        w_fwd.append(forward(w_part(across, 1 - x_pos, j), (dp, mate)))
     for copies, keep in ctx_copies:
-        keep.wait()
-        for copy in copies:
-            copy.wait_recv()
-    mixed[...] = (res_ref[...].astype(F32) + ctx_out[...].astype(F32)).astype(BF)
-    w_self.wait()
-    w_mate.wait_recv()
-    for copy in w_fwd1 + w_fwd2:
+        copies[0].wait_recv()
+        copies[1].wait_recv()
+    mixed[:, far] = (res_v[:, far].astype(F32) + ctx_out[:, far].astype(F32)).astype(BF)
+    for copy in w_fwd:
         copy.wait_recv()
-
-    wide = 2 * LANES
 
     def conv_in(i, carry):
         cols = at(i, wide)
         gates = pl.ds(pl.multiple_of(channels + i * wide, wide), wide)
-        a = jnp.dot(mixed[...], w_full[:, cols], preferred_element_type=F32).astype(BF)
-        b = jnp.dot(mixed[...], w_full[:, gates], preferred_element_type=F32).astype(BF)
+        a = jnp.dot(mixed[:, far], w_full[far, cols], preferred_element_type=F32)
+        b = jnp.dot(mixed[:, far], w_full[far, gates], preferred_element_type=F32)
+        a = (a + pre[:, cols]).astype(BF)
+        b = (b + pre[:, gates]).astype(BF)
         sig = jax.nn.sigmoid(b.astype(F32))
         a_s[:, cols] = a
         sig_s[:, cols] = sig
@@ -396,6 +422,22 @@
         glu_f.at[:, rows : rows + HALO, :], glu_f.at[:, 0:HALO, :], (dp, lax.rem(me + 1, n_seq))
     )
     halo1.start()
+    span = taps - 1
+    base = HALO - span
+
+    def depth_rows(first, count):
+        def body(c, total):
+            lanes = at(c, LANES)
+            acc = jnp.zeros((count, LANES), F32)
+            for o in range(taps):
+                low = base + first + o
+                acc = acc + taps_ref[o : o + 1, lanes] * glu_f[c, low : low + count, :]
+            dw[c, first : first + count, :] = acc
+            return total + acc
+
+        return lax.fori_loop(0, chunks, body, jnp.zeros((count, LANES), F32))
+
+    total_late = depth_rows(HALO, rows - HALO)
     halo1.wait_recv()
     halo1.wait_send()
 
@@ -403,20 +445,13 @@
     def _():
         glu_f[:, 0:HALO, :] = jnp.zeros((chunks, HALO, LANES), F32)
 
-    span = taps - 1
-    base = HALO - span
-
-    def depth_conv(c, total):
-        lanes = at(c, LANES)
-        acc = jnp.zeros((rows, LANES), F32)
-        for o in range(taps):
-            acc = acc + taps_ref[o : o + 1, lanes] * glu_f[c, base + o : base + o + rows, :]
-        dw[c] = acc
-        return total + acc
-
+    total_early = depth_rows(0, HALO)
+    average = jnp.concatenate(
+        [jnp.sum(total_early, axis=1, keepdims=True), jnp.sum(total_late, axis=1, keepdims=True)],
+        axis=0,
+    ) * (1.0 / channels)
     zero = jnp.zeros((rows, LANES), F32)
-    total = lax.fori_loop(0, chunks, depth_conv, zero)
-    average = jnp.sum(total, axis=1, keepdims=True) * (1.0 / channels)
+    loads[2].wait()
 
     def squares(c, total):
         centered = dw[c] - average
@@ -433,7 +468,7 @@
         affine = normed * gain_ref[:, lanes] + bias_ref[:, lanes]
         sig = jax.nn.sigmoid(affine)
         conv_out[:, lanes] = (affine * sig).astype(BF)
-        affine_grad = og_ref[:, lanes].astype(F32) * (sig * (1.0 + affine * (1.0 - sig)))
+        affine_grad = og_v[:, lanes].astype(F32) * (sig * (1.0 + affine * (1.0 - sig)))
         part[c, taps : taps + 1, :] = jnp.sum(affine_grad * normed, axis=0, keepdims=True)
         part[c, taps + 1 : taps + 2, :] = jnp.sum(affine_grad, axis=0, keepdims=True)
         normed_grad = affine_grad * gain_ref[:, lanes]
@@ -454,6 +489,47 @@
         dg.at[:, 0:HALO, :], dg.at[:, rows : rows + HALO, :], (dp, lax.rem(me + n_seq - 1, n_seq))
     )
     halo2.start()
+
+    def glu_back(first, count):
+        def body(c, carry):
+            lanes = at(c, LANES)
+            gates = pl.ds(pl.multiple_of(channels + c * LANES, LANES), LANES)
+            here = slice(first, first + count)
+            acc = jnp.zeros((count, LANES), F32)
+            for o in range(taps):
+                low = first + span - o
+                acc = acc + taps_ref[o : o + 1, lanes] * dg[c, low : low + count, :]
+            sig = sig_s[here, lanes]
+            ig_out[here, lanes] = (acc * sig).astype(BF)
+            slope = acc * a_s[here, lanes].astype(F32) * sig * (1.0 - sig)
+            ig_out[here, gates] = slope.astype(BF)
+            return carry
+
+        lax.fori_loop(0, chunks, body, 0)
+
+    glu_back(0, rows - HALO)
+    halo2.wait_recv()
+    halo2.wait_send()
+
+    @pl.when(me == n_seq - 1)
+    def _():
+        dg[:, rows : rows + HALO, :] = jnp.zeros((chunks, HALO, LANES), F32)
+
+    glu_back(rows - HALO, HALO)
+    loads[1].wait()
+    g_send = []
+    for p in peers + [me]:
+        cols = at(p, own)
+        grad = lax.dot_general(
+            ig_out[...], w_full[cols, :], (((1,), (1,)), ((), ())), preferred_element_type=F32
+        )
+        rg_out[:, cols] = (cg_v[:, cols].astype(F32) + grad).astype(BF)
+        if p is me:
+            g_h[at(me, rows), :] = rg_out[:, cols]
+        else:
+            copy = remote(rg_out.at[:, cols], g_h.at[at(me, rows), :], (dp, p))
+            copy.start()
+            g_send.append(copy)
 
     def tap_grad(c, carry):
         grad = dg[c, 0:rows, :]
@@ -471,57 +547,8 @@
         copy.start()
         reduce1.append(copy)
 
-    halo2.wait_recv()
-    halo2.wait_send()
-
-    @pl.when(me == n_seq - 1)
-    def _():
-        dg[:, rows : rows + HALO, :] = jnp.zeros((chunks, HALO, LANES), F32)
-
-    def glu_back(c, carry):
-        lanes = at(c, LANES)
-        gates = pl.ds(pl.multiple_of(channels + c * LANES, LANES), LANES)
-        acc = jnp.zeros((rows, LANES), F32)
-        for o in range(taps):
-            acc = acc + taps_ref[o : o + 1, lanes] * dg[c, span - o : span - o + rows, :]
-        sig = sig_s[:, lanes]
-        ig_out[:, lanes] = (acc * sig).astype(BF)
-        ig_out[:, gates] = (acc * a_s[:, lanes].astype(F32) * sig * (1.0 - sig)).astype(BF)
-        return carry
-
-    lax.fori_loop(0, chunks, glu_back, 0)
-
-    def mixed_back(i, carry):
-        cols = at(i, wide)
-        grad = lax.dot_general(
-            ig_out[...], w_full[cols, :], (((1,), (1,)), ((), ())), preferred_element_type=F32
-        )
-        rg_out[:, cols] = (cg_ref[:, cols].astype(F32) + grad).astype(BF)
-        return carry
-
-    lax.fori_loop(0, channels // wide, mixed_back, 0)
-    g_send = scatter_heads(rg_out, g_h)
-    g_self = pltpu.make_async_copy(
-        rg_out.at[:, at(me, own)], g_h.at[at(me, rows), :], lsem.at[6]
-    )
-    g_self.start()
-
-    for copy in reduce1:
-        copy.wait_recv()
-    total = part[dp]
-    for d in range(n_dp - 1):
-        total = total + rs_buf[d]
-    s2_buf[me] = total
-    reduce2 = []
-    for p in peers:
-        copy = remote(s2_buf.at[me], s2_buf.at[me], (dp, p))
-        copy.start()
-        reduce2.append(copy)
-
-    g_self.wait()
     for copy in g_send:
         copy.wait_recv()
-    gt[...] = flip(g_h).astype(BF)
 
     def backward_head(h):
         hr = slice(h * depth, (h + 1) * depth)
@@ -536,7 +563,6 @@
             prob_grad = jnp.dot(v_h[:, hr], grad, preferred_element_type=F32)
             p = prob[h, :, cols]
             score_grad = (p * (prob_grad - dots) * scaling).astype(BF)
-            pb_s[slot, :, cols] = p.astype(BF)
             ds_s[slot, :, cols] = score_grad
             dqt[hr, cols] = jnp.dot(kt[hr, :], score_grad, preferred_element_type=F32)
             return carry
@@ -545,33 +571,46 @@
 
     first = lax.broadcasted_iota(jnp.int32, (frames, LANES), 1) < depth
     out_copies = []
-    reduce3 = []
+    reduce2, reduce3 = [], []
+    for pair in range(pairs):
+        pc = slice(pair * LANES, (pair + 1) * LANES)
+        left = jnp.dot(pb_s[2 * pair], g_h[:, pc], preferred_element_type=F32)
+        right = jnp.dot(pb_s[2 * pair + 1], g_h[:, pc], preferred_element_type=F32)
+        dv_h[:, pc] = jnp.where(first, left, right).astype(BF)
+        out_copies.append(gather_pair(dv_h, dv_out, pair, 12 + pair))
+        gt[pc, :] = flip(g_h[:, pc]).astype(BF)
     for pair in range(pairs):
         pc = slice(pair * LANES, (pair + 1) * LANES)
         backward_head(2 * pair)
         backward_head(2 * pair + 1)
         dq_h[:, pc] = dqt[pc, :].T.astype(BF)
-        out_copies.append(gather_pair(dq_h, dq_out, pair, 7 + 3 * pair))
+        out_copies.append(gather_pair(dq_h, dq_out, pair, 14 + 2 * pair))
         left = jnp.dot(ds_s[0], q_h[:, pc], preferred_element_type=F32)
         right = jnp.dot(ds_s[1], q_h[:, pc], preferred_element_type=F32)
         dk_h[:, pc] = jnp.where(first, left, right).astype(BF)
-        out_copies.append(gather_pair(dk_h, dk_out, pair, 8 + 3 * pair))
-        left = jnp.dot(pb_s[0], g_h[:, pc], preferred_element_type=F32)
-        right = jnp.dot(pb_s[1], g_h[:, pc], preferred_element_type=F32)
-        dv_h[:, pc] = jnp.where(first, left, right).astype(BF)
-        out_copies.append(gather_pair(dv_h, dv_out, pair, 9 + 3 * pair))
+        out_copies.append(gather_pair(dk_h, dk_out, pair, 15 + 2 * pair))
         if pair == 0:
-            for copy in reduce2:
+            for copy in reduce1:
                 copy.wait_recv()
-            total = s2_buf[0]
-            for s in range(1, n_seq):
-                total = total + s2_buf[s]
-            fin[dp] = total * (1.0 / n_dp)
-            for p in dp_peers:
-                copy = remote(fin.at[dp], fin.at[dp], (p, me))
+            total = part[dp]
+            for d in range(n_dp - 1):
+                total = total + rs_buf[d]
+            s2_buf[me] = total
+            for p in peers:
+                copy = remote(s2_buf.at[me], s2_buf.at[me], (dp, p))
                 copy.start()
-                reduce3.append(copy)
-
+                reduce2.append(copy)
+
+    for copy in reduce2:
+        copy.wait_recv()
+    total = s2_buf[0]
+    for s in range(1, n_seq):
+        total = total + s2_buf[s]
+    fin[dp] = total * (1.0 / n_dp)
+    for p in dp_peers:
+        copy = remote(fin.at[dp], fin.at[dp], (p, me))
+        copy.start()
+        reduce3.append(copy)
     for copy in reduce3:
         copy.wait_recv()
     for c in range(chunks):
@@ -584,13 +623,22 @@
         keep.wait()
         for copy in copies:
             copy.wait_recv()
-    for copies in sends + [c for c, _ in ctx_copies] + [c for c, _ in out_copies]:
+    for copies, _ in sends + ctx_copies + out_copies:
         for copy in copies:
             copy.wait_send()
     for copy in (
-        [w_mate] + w_across + w_x + w_fwd1 + w_fwd2 + g_send + reduce1 + reduce2 + reduce3
+        [w_mate] + w_across + w_x + w_fwd + g_send + reduce1 + reduce2 + reduce3
     ):
         copy.wait_send()
+
+
+def place_outputs(*refs):
+    sems = refs[20]
+    copies = [pltpu.make_async_copy(refs[i], refs[10 + i], sems.at[i]) for i in range(10)]
+    for copy in copies:
+        copy.start()
+    for copy in copies:
+        copy.wait()
 
 
 def fused_shards(
@@ -611,13 +659,17 @@
     block = s((rows, channels), BF)
     head_rows = vm((frames, own), BF)
     head_cols = vm((own, frames), BF)
-    n_copies = 96
+    n_copies = 112
     scratch = (
         [head_rows] * 4 + [head_cols] * 5 + [head_rows]
-        + [vm((heads, frames, frames), F32), vm((2, frames, frames), BF), vm((2, frames, frames), BF)]
+        + [vm((heads, frames, frames), F32), vm((heads, frames, frames), BF), vm((2, frames, frames), BF)]
         + [vm((own, frames), F32)] + [head_rows] * 3
         + [
+            vm((rows, channels), BF),
+            vm((rows, channels), BF),
+            vm((rows, channels), BF),
             vm((channels, 2 * channels), BF),
+            vm((rows, 2 * channels), F32),
             vm((rows, channels), BF),
             vm((rows, channels), BF),
             vm((rows, channels), F32),
@@ -631,17 +683,18 @@
             vm((chunks, TERM_ROWS, LANES), F32),
             pltpu.SemaphoreType.DMA((n_copies,)),
             pltpu.SemaphoreType.DMA((n_copies,)),
-            pltpu.SemaphoreType.DMA((16,)),
+            pltpu.SemaphoreType.DMA((20,)),
         ]
     )
     spec = pl.BlockSpec(memory_space=pltpu.VMEM)
+    hbm = pl.BlockSpec(memory_space=pl.ANY)
     outs = pl.pallas_call(
         functools.partial(fused_kernel, (n_seq, n_dp, rows, channels, taps, depth)),
         out_shape=(
             block, block, block, block, block, s((rows, 2 * channels), BF), block,
             s((taps, channels), F32), s((1, channels), F32), s((1, channels), F32),
         ),
-        in_specs=[spec] * 10,
+        in_specs=[hbm] * 6 + [spec] * 3 + [hbm],
         out_specs=(spec,) * 10,
         scratch_shapes=scratch,
         compiler_params=pltpu.CompilerParams(
@@ -651,6 +704,13 @@
         queries[0], key_vecs[0], value_vecs[0], residual_in[0], point_weight, context_grad[0],
         depth_kernel, norm_gain[None], norm_bias[None], conv_grad[0],
     )
+    outs = pl.pallas_call(
+        place_outputs,
+        out_shape=tuple(s(o.shape, o.dtype) for o in outs),
+        in_specs=[hbm] * 10,
+        out_specs=(hbm,) * 10,
+        scratch_shapes=[pltpu.SemaphoreType.DMA((10,))],
+    )(*outs)
     return tuple(o[None] for o in outs[:7]) + (outs[7], outs[8][0], outs[9][0])
 
 
@@ -666,7 +726,8 @@
         and 2 * channels == LANES * HEADS
         and channels // LANES == n_dp
         and rows * n_seq <= 512
-        and args[6].shape[0] <= 32
+        and args[4].shape[0] == channels // n_seq == 2 * LANES
+        and args[6].shape[0] <= 31
     )
     return fused_shards(*args) if fits else shards(*args)
 

time: 82 us -> 139 us (1.70)
  Pallas kernels: 71.8 us -> 138 us
  local copies, waits for them, and re-layouts: 9.23 us -> 0 us
    pallas_call x0 -> x1, Pallas kernels: none -> 68.9 us  [fused_shards(): pl.pallas_call(place_outputs, out_shape=tuple((s(o.shape, o.dtype) for o...]
    unnamed x28 -> x0, local copies, waits for them, and re-layouts: 9.23 us -> none
    pallas_call x1, Pallas kernels: 71.8 us -> 69.2 us  [fused_shards(): pl.pallas_call(functools.partial(fused_kernel, (n_seq, n_dp, rows, channe...]
where the time goes in v2:
time: 139 us
  Pallas kernels  138 us (99%)
    pallas_call x1, Pallas kernels, fused_shards(): pl.pallas_call(functools.partial(fused_kernel, (n_seq, n_dp, rows, channe...  69.2 us
    pallas_call x1, Pallas kernels, fused_shards(): pl.pallas_call(place_outputs, out_shape=tuple((s(o.shape, o.dtype) for o...  68.9 us

profile of v2, /device:TPU:0, one launch (start us, length us, event | category | flops | bytes accessed | tf_op | source)
XLA Modules:
  0.0 138.8 jit_solution(2452820436163544400)
XLA Ops:
  0.6 69.2 %shard_map.177 = (bf16[128,1024]{1,0:T(8,128)(2,1)}, bf16[128,1024]{1,0:T(8,128)(2,1)}, bf16[128,1024]{1,0:T(8,128)(2,1)}, bf16[128,1024]{1,0:T(8,128)(2,1)}, bf...) custom-call(bf16[128,1024]{1,0:T(8,128)(2,1)} %bitcast.17, ...), custom_call_target="tpu_custom_call" | custom-call | tf_op jit(solution)/shard_map/pallas_call | solution.py:691
  69.9 68.9 %shard_map.178 = (bf16[128,1024]{1,0:T(8,128)(2,1)}, bf16[128,1024]{1,0:T(8,128)(2,1)}, bf16[128,1024]{1,0:T(8,128)(2,1)}, bf16[128,1024]{1,0:T(8,128)(2,1)}, bf...) custom-call(bf16[128,1024]{1,0:T(8,128)(2,1)} %get-tuple-element.30., ...), custom_call_target="tpu_custom_call" | custom-call | tf_op jit(solution)/shard_map/pallas_call | solution.py:707

commit v3 on v2

--- a/solution.py
+++ b/solution.py
@@ -286,7 +286,7 @@
 
     w_rows = w_ref.shape[0]
     half = w_rows // 2
-    pieces = 2
+    pieces = 4
     piece = half // pieces
     w_mate = remote(w_ref, w_full.at[at(me, w_rows), :], (dp, mate))
     w_mate.start()
@@ -579,6 +579,16 @@
         dv_h[:, pc] = jnp.where(first, left, right).astype(BF)
         out_copies.append(gather_pair(dv_h, dv_out, pair, 12 + pair))
         gt[pc, :] = flip(g_h[:, pc]).astype(BF)
+    for copy in reduce1:
+        copy.wait_recv()
+    total = part[dp]
+    for d in range(n_dp - 1):
+        total = total + rs_buf[d]
+    s2_buf[me] = total
+    for p in peers:
+        copy = remote(s2_buf.at[me], s2_buf.at[me], (dp, p))
+        copy.start()
+        reduce2.append(copy)
     for pair in range(pairs):
         pc = slice(pair * LANES, (pair + 1) * LANES)
         backward_head(2 * pair)
@@ -590,27 +600,17 @@
         dk_h[:, pc] = jnp.where(first, left, right).astype(BF)
         out_copies.append(gather_pair(dk_h, dk_out, pair, 15 + 2 * pair))
         if pair == 0:
-            for copy in reduce1:
+            for copy in reduce2:
                 copy.wait_recv()
-            total = part[dp]
-            for d in range(n_dp - 1):
-                total = total + rs_buf[d]
-            s2_buf[me] = total
-            for p in peers:
-                copy = remote(s2_buf.at[me], s2_buf.at[me], (dp, p))
+            total = s2_buf[0]
+            for s in range(1, n_seq):
+                total = total + s2_buf[s]
+            fin[dp] = total * (1.0 / n_dp)
+            for p in dp_peers:
+                copy = remote(fin.at[dp], fin.at[dp], (p, me))
                 copy.start()
-                reduce2.append(copy)
-
-    for copy in reduce2:
-        copy.wait_recv()
-    total = s2_buf[0]
-    for s in range(1, n_seq):
-        total = total + s2_buf[s]
-    fin[dp] = total * (1.0 / n_dp)
-    for p in dp_peers:
-        copy = remote(fin.at[dp], fin.at[dp], (p, me))
-        copy.start()
-        reduce3.append(copy)
+                reduce3.append(copy)
+
     for copy in reduce3:
         copy.wait_recv()
     for c in range(chunks):
@@ -707,7 +707,7 @@
     outs = pl.pallas_call(
         place_outputs,
         out_shape=tuple(s(o.shape, o.dtype) for o in outs),
-        in_specs=[hbm] * 10,
+        in_specs=[spec] * 10,
         out_specs=(hbm,) * 10,
         scratch_shapes=[pltpu.SemaphoreType.DMA((10,))],
     )(*outs)

time: 139 us -> 71.2 us (0.51)
  Pallas kernels: 138 us -> 70.3 us
    pallas_call x1, Pallas kernels: 68.9 us -> 3 us  [fused_shards(): pl.pallas_call(place_outputs, out_shape=tuple((s(o.shape, o.dtype) for o...]
    pallas_call x1, Pallas kernels: 69.2 us -> 67.3 us  [fused_shards(): pl.pallas_call(functools.partial(fused_kernel, (n_seq, n_dp, rows, channe...]
where the time goes in v3:
time: 71.2 us; the launch traced here: 71 us
  Pallas kernels  70.3 us (99%)
    pallas_call x1, Pallas kernels, fused_shards(): pl.pallas_call(functools.partial(fused_kernel, (n_seq, n_dp, rows, channe...  67.3 us
    pallas_call x1, Pallas kernels, fused_shards(): pl.pallas_call(place_outputs, out_shape=tuple((s(o.shape, o.dtype) for o...  3 us

profile of v3, /device:TPU:0, one launch (start us, length us, event | category | flops | bytes accessed | tf_op | source)
XLA Modules:
  0.0 71.0 jit_solution(4043109601021090592)
XLA Ops:
  0.6 67.3 %shard_map.177 = (bf16[128,1024]{1,0:T(8,128)(2,1)}, bf16[128,1024]{1,0:T(8,128)(2,1)}, bf16[128,1024]{1,0:T(8,128)(2,1)}, bf16[128,1024]{1,0:T(8,128)(2,1)}, bf...) custom-call(bf16[128,1024]{1,0:T(8,128)(2,1)} %bitcast.17, ...), custom_call_target="tpu_custom_call" | custom-call | tf_op jit(solution)/shard_map/pallas_call | solution.py:691
  68.0 3.0 %shard_map.178 = (bf16[128,1024]{1,0:T(8,128)(2,1)}, bf16[128,1024]{1,0:T(8,128)(2,1)}, bf16[128,1024]{1,0:T(8,128)(2,1)}, bf16[128,1024]{1,0:T(8,128)(2,1)}, bf...) custom-call(bf16[128,1024]{1,0:T(8,128)(2,1)} %get-tuple-element.30., ...), custom_call_target="tpu_custom_call" | custom-call | tf_op jit(solution)/shard_map/pallas_call | solution.py:707
